TPU v7x, 256 devices: a whole 4x4x8 slice. The times are simulated.
256 devices in a mesh: dp: 128 (over y, z, x), rep: 2 (over core).
Axes of the slice: x: 4, y: 4, z: 8, core: 2. Of those that a mesh axis runs over, the one named last changes fastest.
Arguments:
- embeddings: float32 [131072, 1024], P(('dp', 'rep')), may hold values from -6 to 6
- cluster_ids: int32 [131072, 1], P(('dp', 'rep')), may hold values from 0 to 255; in each aligned block of 512 rows (0 to 511, 512 to 1023, ...) at most 4 rows name the same one
- boundary_slots: int32 [256, 2, 256], P(('dp', 'rep')), may hold values from 0 to 1023
Outputs:
- member_max: float32 [256, 1024], P(('dp', 'rep'))
- centrality: float32 [256, 1024], P(('dp', 'rep'))
Inputs may be any that keep to these rules, and one draw needn't show every extreme that they name: `cluster_ids`: among the rows of one device, at most 4 name the same cluster, a bound that some block reaches of them; every cluster is named by some row.
All inputs are finite; a program needn't handle non-finite values.
Results may differ from a plain program's by a relative error of at most 0.0024.
Values may be sent and summed in bfloat16 or wider, within the bound.
A program may use at most 64 MiB of HBM per device.

v0:
```python
import jax
import jax.numpy as jnp
from jax import lax
from jax.sharding import PartitionSpec as P

SLOTS = 1024
eps = 1e-06


def from_behind(array, axis, by):
    peers = lax.axis_size(axis)
    pairs = [(i, i + by) for i in range(peers) if 0 <= i + by < peers]
    return lax.ppermute(array, axis, pairs)


def per_device(embeddings, cluster_ids, boundary_slots):
    n_chips = lax.axis_size("dp")
    n_cores = lax.axis_size("rep")
    owners = n_chips * n_cores
    width = embeddings.shape[1]
    slots = SLOTS
    capacity = slots // owners
    bound = boundary_slots.shape[2]
    me = lax.axis_index(("dp", "rep"))
    labels = cluster_ids[:, 0]
    member_of = labels[:, None] == jnp.arange(owners, dtype=jnp.int32)[None, :]
    running = jnp.cumsum(member_of.astype(jnp.int32), axis=0)
    ranks = jnp.sum(jnp.where(member_of, running, 0), axis=1) - 1
    targets = labels * capacity + ranks
    unit_full = embeddings * lax.rsqrt(
        jnp.sum(embeddings * embeddings, axis=1, keepdims=True) + eps
    )
    unit_half = unit_full.astype(jnp.bfloat16)
    outgoing = jnp.zeros((slots, width), jnp.bfloat16).at[targets].set(unit_half)
    shaped = outgoing.reshape(n_chips, n_cores, capacity, width)
    arrived = lax.all_to_all(
        lax.all_to_all(shaped, "dp", split_axis=0, concat_axis=0, tiled=True),
        "rep",
        split_axis=1,
        concat_axis=1,
        tiled=True,
    )
    members = arrived.reshape(slots, width)
    own_sum = lax.dot_general(
        jnp.ones((1, slots), jnp.bfloat16),
        members,
        (((1,), (0,)), ((), ())),
        preferred_element_type=jnp.float32,
    )
    direction = own_sum[0] * lax.rsqrt(jnp.sum(own_sum * own_sum) + eps)
    lengths = jnp.einsum("se,se->s", members, members, preferred_element_type=jnp.float32)
    filled = lengths > 0.5
    filled_int = filled.astype(jnp.int32)
    count = jnp.sum(filled_int)
    order = jnp.argsort(1 - filled_int, stable=True)
    picks = boundary_slots[0] % count
    positions = order[picks.reshape(-1)]
    outward = members[positions]
    lower = from_behind(outward[bound:], ("dp", "rep"), 1)
    upper = from_behind(outward[:bound], ("dp", "rep"), -1)
    candidates = jnp.concatenate([members, lower, upper], axis=0)
    cand_ok = jnp.concatenate(
        [filled, jnp.full((bound,), me > 0), jnp.full((bound,), me < owners - 1)]
    )
    column = jnp.arange(slots + 2 * bound, dtype=jnp.int32)
    block = min(512, slots)

    def one_block(start):
        block_rows = lax.dynamic_slice_in_dim(members, start, block, 0)
        scores = lax.dot_general(
            block_rows, candidates, (((1,), (1,)), ((), ())), preferred_element_type=jnp.float32
        )
        row_pos = start + jnp.arange(block, dtype=jnp.int32)
        keep = cand_ok[None, :] & (column[None, :] != row_pos[:, None])
        return jnp.max(jnp.where(keep, scores, -1.0), axis=1)

    starts = jnp.arange(slots // block, dtype=jnp.int32) * block
    best = lax.map(one_block, starts).reshape(slots)
    member_max = jnp.where(filled, best, 0.0)
    central = jnp.dot(
        members, direction, precision=lax.Precision.HIGHEST, preferred_element_type=jnp.float32
    )
    centrality = jnp.where(filled, central, 0.0)
    return (member_max[None, :], centrality[None, :])


def solution(mesh):
    placed = (P(("dp", "rep"), None), P(("dp", "rep"), None), P(("dp", "rep"), None, None))
    return jax.shard_map(
        per_device,
        mesh=mesh,
        in_specs=placed,
        out_specs=(P(("dp", "rep"), None), P(("dp", "rep"), None)),
        check_vma=False,
    )
```

profile of v0, /device:TPU:7, one launch (start us, length us, event | category | flops | bytes accessed | tf_op | source)
XLA Modules:
  0.0 137.3 jit_solution(18101900111716776001)
XLA Ops:
  0.6 0.9 copy.12
  2.5 4.2 %scatter_custom_fusion = bf16[1024,1024]{1,0:T(8,128)(2,1)} fusion(s32[512]{0:T(512)S(1)} %bitcast.60, f32[512,1024]{1,0:T(8,128)S(1)} %copy-done, f32[512]{0:T(512)S(1)} %add_rsqrt_fusion, bf16[]{:T(256)} %constant.27.clone.1), kind=kCustom, calls=%fused_computation.16 | custom fusion | flops 1048576 | bytes 4196354 | tf_op jit(solution)/shard_map/scatter | solution.py:34
  6.7 2.7 %reshape.111 = bf16[128,2,4,1024]{3,2,1,0:T(4,128)(2,1)S(1)} reshape(bf16[1024,1024]{1,0:T(8,128)(2,1)} %scatter_custom_fusion) | data formatting | bytes 4194304 | tf_op jit(solution)/shard_map/reshape | solution.py:35
  9.5 64.2 %all_to_all.10 = bf16[128,2,4,1024]{3,2,1,0:T(4,128)(2,1)S(1)} all-to-all(bf16[128,2,4,1024]{3,2,1,0:T(4,128)(2,1)S(1)} %reshape.111), channel_id=1, replica_groups=mesh['dp'=128,'rep'=2] {'dp'}, dimensions={0} | all-to-all | bytes 4194304 | tf_op jit(solution)/shard_map/all_to_all | solution.py:37
  73.6 0.7 copy.14
  74.4 8.0 %all_to_all.11 = bf16[128,2,4,1024]{3,2,0,1:T(4,128)(2,1)S(1)} all-to-all(bf16[128,2,4,1024]{3,2,0,1:T(4,128)(2,1)S(1)} %copy.14), channel_id=1, replica_groups=mesh['dp'=128,'rep'=2] {'rep'}, dimensions={1} | all-to-all | bytes 4194304 | tf_op jit(solution)/shard_map/all_to_all | solution.py:36
  82.3 2.6 %copy.15 = bf16[128,2,4,1024]{3,2,1,0:T(4,128)(2,1)} copy(bf16[128,2,4,1024]{3,2,0,1:T(4,128)(2,1)S(1)} %all_to_all.11) | data formatting | bytes 4194304 | tf_op jit(solution)/shard_map/all_to_all | solution.py:36
  85.0 2.5 %reshape.112 = bf16[1024,1024]{1,0:T(8,128)(2,1)S(1)} reshape(bf16[128,2,4,1024]{3,2,1,0:T(4,128)(2,1)} %copy.15) | data formatting | bytes 4194304 | tf_op jit(solution)/shard_map/reshape | solution.py:43
  88.4 0.6 multiply_reduce_fusion.1
  89.7 1.7 %fusion.18 = f32[1,1024]{1,0:T(1,128)S(1)} fusion(bf16[1024,1024]{1,0:T(8,128)(2,1)S(1)} %reshape.112, f32[1024,1]{0,1:T(1,128)S(1)} %bitcast.50), kind=kOutput, calls=%fused_computation.50 | convolution fusion | flops 12582912 | bytes 2105344 | tf_op jit(solution)/shard_map/dot_general | solution.py:80
  91.4 0.6 broadcast_select_fusion
  92.0 0.6 convert_reduce_fusion
  94.1 4.4 %sort.17 = (s32[1024]{0:T(1024)}, s32[1024]{0:T(1024)S(1)}) sort(s32[1024]{0:T(1024)S(1)} %get-tuple-element.73, s32[1024]{0:T(1024)S(1)} %iota.25), dimensions={0}, to_apply=%region_5.6 | sort | flops 10240 | bytes 16384 | tf_op jit(solution)/shard_map/jit(argsort)/sort | solution.py:55
  98.5 2.3 %gather_fusion = s32[512]{0:T(512)S(1)} fusion(s32[1024]{0:T(1024)S(1)} %get-tuple-element.40, s32[1024]{0:T(1024)S(1)} %pad_clamp_fusion.1), kind=kCustom, calls=%fused_computation | custom fusion | bytes 6144 | tf_op jit(solution)/shard_map/gather | solution.py:57
  100.8 2.1 %gather_fusion.1 = bf16[512,1024]{1,0:T(8,128)(2,1)S(1)} fusion(bf16[1024,1024]{1,0:T(8,128)(2,1)S(1)} %reshape.112, s32[1024]{0:T(1024)S(1)} %pad_clamp_fusion), kind=kCustom, calls=%fused_computation.1 | custom fusion | bytes 2099200 | tf_op jit(solution)/shard_map/gather | solution.py:58
  102.9 1.1 fusion.17
  103.9 4.4 %collective-permute-start = (bf16[256,1024]{1,0:T(8,128)(2,1)}, bf16[256,1024]{1,0:T(8,128)(2,1)S(1)}, u32[]{:S(2)}, u32[]{:S(2)}) collective-permute-start(bf16[256,1024]{1,0:T(8,128)(2,1)} %get-tuple-element.70), channel_id=1, source_target_pairs={{0,1},{1,2},{2,3},{3,4},{4,5},{5,6},{6,7},{7,8},{8,9},{9,10},{10,1... | collective-permute-start | bytes 1572872 | tf_op jit(solution)/shard_map/ppermute | solution.py:13
  108.3 1.9 %collective-permute-start.1 = (bf16[256,1024]{1,0:T(8,128)(2,1)}, bf16[256,1024]{1,0:T(8,128)(2,1)S(1)}, u32[]{:S(2)}, u32[]{:S(2)}) collective-permute-start(bf16[256,1024]{1,0:T(8,128)(2,1)} %get-tuple-element.71), channel_id=1, source_target_pairs={{1,0},{2,1},{3,2},{4,3},{5,4},{6,5},{7,6},{8,7},{9,8},{10,9},{11,1... | collective-permute-start | bytes 1572872 | tf_op jit(solution)/shard_map/ppermute | solution.py:13
  110.3 4.4 %collective-permute-done = bf16[256,1024]{1,0:T(8,128)(2,1)S(1)} collective-permute-done((bf16[256,1024]{1,0:T(8,128)(2,1)}, bf16[256,1024]{1,0:T(8,128)(2,1)S(1)}, u32[]{:S(2)}, u32[]{:S(2)}) %collective-permute-start) | collective-permute-done | bytes 524320 | tf_op jit(solution)/shard_map/ppermute | solution.py:13
  114.8 6.4 %collective-permute-done.1 = bf16[256,1024]{1,0:T(8,128)(2,1)S(1)} collective-permute-done((bf16[256,1024]{1,0:T(8,128)(2,1)}, bf16[256,1024]{1,0:T(8,128)(2,1)S(1)}, u32[]{:S(2)}, u32[]{:S(2)}) %collective-permute-start.1) | collective-permute-done | bytes 524320 | tf_op jit(solution)/shard_map/ppermute | solution.py:13
  121.2 1.9 %pad_maximum_fusion = bf16[1536,1024]{1,0:T(8,128)(2,1)} fusion(bf16[256,1024]{1,0:T(8,128)(2,1)S(1)} %collective-permute-done.1, bf16[256,1024]{1,0:T(8,128)(2,1)S(1)} %collective-permute-done, bf16[1024,1024]{1,0:T(8,128)(2,1)S(1)} %reshape.112), kind=kLoop, calls=%fused_computation.13 | loop fusion | flops 9437184 | bytes 6291456 | tf_op jit(solution)/shard_map/concatenate | solution.py:61
  123.1 13.6 %while.11 = (s32[]{:T(128)}, f32[2,512]{1,0:T(2,128)S(1)}, pred[1536]{0:T(1024)(128)(4,1)S(1)}, s32[2]{0:T(128)S(1)}, bf16[1024,1024]{1,0:T(8,128)(2,1)S(1)}, /*...) while((s32[]{:T(128)}, f32[2,512]{1,0:T(2,128)S(1)}, ...), condition=%wide.region_9.10_spmd.clone, body=%wide.region_7.9_spmd.clone.sunk | while | flops 1613758464 | bytes 4206743 | solution.py:78
  125.8 4.0 %fusion.28 = f32[512]{0:T(512)S(1)} fusion(bf16[1536,1024]{1,0:T(8,128)(2,1)} %get-tuple-element.134, s32[512]{0:T(512)S(1)} %iota_add_fusion.2, pred[1536]{0:T(1024)(128)(4,1)S(1)} %get-tuple-element.131, bf16[1024,1024]{1,0:T(8,128)(2,1)S(1)} %get-tuple-element.133, s32[]{:T(128)S(6)} %select_n.86), kind=kOutput, calls=%fused_computation.7.clone.1 | convolution fusion | flops 1613757952 | bytes 4200452 | tf_op jit(solution)/shard_map/while/body/eval_jaxpr/dot_general | solution.py:70
  132.6 4.0 %fusion.28 = f32[512]{0:T(512)S(1)} fusion(bf16[1536,1024]{1,0:T(8,128)(2,1)} %get-tuple-element.134, s32[512]{0:T(512)S(1)} %iota_add_fusion.2, pred[1536]{0:T(1024)(128)(4,1)S(1)} %get-tuple-element.131, bf16[1024,1024]{1,0:T(8,128)(2,1)S(1)} %get-tuple-element.133, s32[]{:T(128)S(6)} %select_n.86), kind=kOutput, calls=%fused_computation.7.clone.1 | convolution fusion | flops 1613757952 | bytes 4200452 | tf_op jit(solution)/shard_map/while/body/eval_jaxpr/dot_general | solution.py:70
  (41 shorter events, 4.8 us)
Async XLA Ops:
  0.6 1.4 %copy-start.1 = (s32[512,1]{0,1:T(1,128)S(1)}, s32[512,1]{0,1:T(1,128)}, u32[]{:S(2)}) copy-start(s32[512,1]{0,1:T(1,128)} %param.6) | copy-start | bytes 6148
  0.6 1.6 %copy-start = (f32[512,1024]{1,0:T(8,128)S(1)}, f32[512,1024]{1,0:T(8,128)}, u32[]{:S(2)}) copy-start(f32[512,1024]{1,0:T(8,128)} %param.5) | copy-start | bytes 6291460
  87.9 6.1 %copy-start.2 = (s32[1,2,256]{2,1,0:T(2,128)S(1)}, s32[1,2,256]{2,1,0:T(2,128)}, u32[]{:S(2)}) copy-start(s32[1,2,256]{2,1,0:T(2,128)} %param.7) | copy-start | bytes 6148
  103.9 10.8 %collective-permute-start = (bf16[256,1024]{1,0:T(8,128)(2,1)}, bf16[256,1024]{1,0:T(8,128)(2,1)S(1)}, u32[]{:S(2)}, u32[]{:S(2)}) collective-permute-start(bf16[256,1024]{1,0:T(8,128)(2,1)} %get-tuple-element.70), channel_id=1, source_target_pairs={{0,1},{1,2},{2,3},{3,4},{4,5},{5,6},{6,7},{7,8},{8,9},{9,10},{10,1... | collective-permute-start | bytes 1572872 | tf_op jit(solution)/shard_map/ppermute | solution.py:13
  108.3 12.8 %collective-permute-start.1 = (bf16[256,1024]{1,0:T(8,128)(2,1)}, bf16[256,1024]{1,0:T(8,128)(2,1)S(1)}, u32[]{:S(2)}, u32[]{:S(2)}) collective-permute-start(bf16[256,1024]{1,0:T(8,128)(2,1)} %get-tuple-element.71), channel_id=1, source_target_pairs={{1,0},{2,1},{3,2},{4,3},{5,4},{6,5},{7,6},{8,7},{9,8},{10,9},{11,1... | collective-permute-start | bytes 1572872 | tf_op jit(solution)/shard_map/ppermute | solution.py:13
where the time goes:
time: 138 us; the launch traced here: 137 us
  blocking collectives  72.1 us (52%)
  local copies, waits for them, and re-layouts  16.3 us (12%)
  other arithmetic  15.4 us (11%)
  waiting for transfers between devices  10.8 us (8%)
  matrix products  10.1 us (7%)
  starting transfers between devices  6.31 us (5%)
  loops' own time  3.3 us (2%)
  between operations  2.89 us (2%)
    all_to_all x1, blocking collectives, per_device(): lax.all_to_all(shaped, 'dp', split_axis=0, concat_axis=0, tiled=True)  64.2 us
    ppermute x2, waiting for transfers between devices, from_behind(): return lax.ppermute(array, axis, pairs)  10.8 us
    dot_general x2, matrix products, one_block(): lax.dot_general(block_rows, candidates, (((1,), (1,)), ((), ())), preferr...  8.02 us
    all_to_all x1, blocking collectives, per_device(): lax.all_to_all(lax.all_to_all(shaped, 'dp', split_axis=0, concat_axis=0,...  7.97 us
    ppermute x2, starting transfers between devices, from_behind(): return lax.ppermute(array, axis, pairs)  6.31 us
    sort x1, other arithmetic, per_device(): order = jnp.argsort(1 - filled_int, stable=True)  4.37 us
    scatter x1, other arithmetic, per_device(): jnp.zeros((slots, width), jnp.bfloat16).at[targets].set(unit_half)  4.22 us
    another operation x1, loops' own time, per_device(): best = lax.map(one_block, starts).reshape(slots)  3.3 us
  transfers between devices with their start and end apart: 2, of which 2 were waited for; matrix products, arithmetic and copies ran while one was open for 0% of the time, Pallas kernels for 0%

commit v1 on v0

--- a/solution.py
+++ b/solution.py
@@ -1,3 +1,4 @@
+import functools
 import jax
 import jax.numpy as jnp
 from jax import lax
@@ -5,6 +6,15 @@
 
 SLOTS = 1024
 eps = 1e-06
+
+
+def cover_the_body(xs, across):
+    response = jnp.split(xs, lax.axis_size(across), axis=1)
+    x_new = lax.all_to_all(jnp.stack(response), across, 0, 0)
+    return jnp.concatenate(x_new, 1)
+
+
+state_step_on = functools.partial(cover_the_body, across="rep")
 
 
 def from_behind(array, axis, by):
@@ -33,13 +43,7 @@
     unit_half = unit_full.astype(jnp.bfloat16)
     outgoing = jnp.zeros((slots, width), jnp.bfloat16).at[targets].set(unit_half)
     shaped = outgoing.reshape(n_chips, n_cores, capacity, width)
-    arrived = lax.all_to_all(
-        lax.all_to_all(shaped, "dp", split_axis=0, concat_axis=0, tiled=True),
-        "rep",
-        split_axis=1,
-        concat_axis=1,
-        tiled=True,
-    )
+    arrived = state_step_on(lax.all_to_all(shaped, "dp", split_axis=0, concat_axis=0, tiled=True))
     members = arrived.reshape(slots, width)
     own_sum = lax.dot_general(
         jnp.ones((1, slots), jnp.bfloat16),

time: 138 us -> 139 us (level)
  other arithmetic: 15.4 us -> 16.9 us
    all_to_all x2 -> x0, local copies, waits for them, and re-layouts: 3.35 us -> none  [the longest x1 2.63 us: per_device(): lax.all_to_all(lax.all_to_all(shaped, 'dp', split_axis=0, concat_axis=0,...]
    another operation x3 -> x5, local copies, waits for them, and re-layouts: 0.11 us -> 3.37 us  [the longest x1 2.54 us: per_device(): members = arrived.reshape(slots, width)]
    another operation x3 -> x4, other arithmetic: 0.27 us -> 1.76 us  [the longest x1 1.48 us: cover_the_body(): x_new = lax.all_to_all(jnp.stack(response), across, 0, 0)]
where the time goes in v1:
time: 139 us
  blocking collectives  72.2 us (52%)
  other arithmetic  16.9 us (12%)
  local copies, waits for them, and re-layouts  16.3 us (12%)
  waiting for transfers between devices  10.8 us (8%)
  matrix products  10.1 us (7%)
  starting transfers between devices  6.26 us (5%)
  loops' own time  3.3 us (2%)
  between operations  2.9 us (2%)
    all_to_all x1, blocking collectives, per_device(): lax.all_to_all(shaped, 'dp', split_axis=0, concat_axis=0, tiled=True)  64.2 us
    ppermute x2, waiting for transfers between devices, from_behind(): return lax.ppermute(array, axis, pairs)  10.8 us
    all_to_all x1, blocking collectives, cover_the_body(): x_new = lax.all_to_all(jnp.stack(response), across, 0, 0)  8.02 us
    dot_general x2, matrix products, one_block(): lax.dot_general(block_rows, candidates, (((1,), (1,)), ((), ())), preferr...  8.02 us
    ppermute x2, starting transfers between devices, from_behind(): return lax.ppermute(array, axis, pairs)  6.26 us
    sort x1, other arithmetic, per_device(): order = jnp.argsort(1 - filled_int, stable=True)  4.37 us
    scatter x1, other arithmetic, per_device(): jnp.zeros((slots, width), jnp.bfloat16).at[targets].set(unit_half)  4.22 us
    another operation x1, loops' own time, per_device(): best = lax.map(one_block, starts).reshape(slots)  3.3 us
  transfers between devices with their start and end apart: 2, of which 2 were waited for; matrix products, arithmetic and copies ran while one was open for 0% of the time, Pallas kernels for 0%

profile of v1, /device:TPU:7, one launch (start us, length us, event | category | flops | bytes accessed | tf_op | source)
XLA Modules:
  0.0 138.8 jit_solution(4149091080611865029)
XLA Ops:
  0.6 0.9 copy.7
  2.5 4.2 %scatter_custom_fusion = bf16[1024,1024]{1,0:T(8,128)(2,1)} fusion(s32[512]{0:T(512)S(1)} %bitcast.70, f32[512,1024]{1,0:T(8,128)S(1)} %copy-done, f32[512]{0:T(512)S(1)} %add_rsqrt_fusion, bf16[]{:T(256)} %constant.27.clone.1), kind=kCustom, calls=%fused_computation.17 | custom fusion | flops 1048576 | bytes 4196354 | tf_op jit(solution)/shard_map/scatter | solution.py:44
  6.7 2.7 %reshape.111 = bf16[128,2,4,1024]{3,2,1,0:T(4,128)(2,1)S(1)} reshape(bf16[1024,1024]{1,0:T(8,128)(2,1)} %scatter_custom_fusion) | data formatting | bytes 4194304 | tf_op jit(solution)/shard_map/reshape | solution.py:45
  9.5 64.2 %all_to_all.10 = bf16[128,2,4,1024]{3,2,1,0:T(4,128)(2,1)S(1)} all-to-all(bf16[128,2,4,1024]{3,2,1,0:T(4,128)(2,1)S(1)} %reshape.111), channel_id=1, replica_groups=mesh['dp'=128,'rep'=2] {'dp'}, dimensions={0} | all-to-all | bytes 4194304 | tf_op jit(solution)/shard_map/all_to_all | solution.py:46
  73.6 0.7 slice_bitcast_fusion.1
  74.4 1.5 %pad_maximum_fusion.1 = bf16[2,128,1,4,1024]{4,3,1,2,0:T(4,128)(2,1)S(1)} fusion(bf16[1,128,1,4,1024]{4,3,1,2,0:T(4,128)(2,1)S(1)} %get-tuple-element.71, bf16[1,128,1,4,1024]{4,3,1,2,0:T(4,128)(2,1)S(1)} %get-tuple-element.70), kind=kLoop, calls=%fused_computation.14 | loop fusion | flops 1048576 | bytes 4194304 | tf_op jit(solution)/shard_map/stack | solution.py:13
  75.8 8.0 %all_to_all.11 = bf16[2,128,1,4,1024]{4,3,1,2,0:T(4,128)(2,1)S(1)} all-to-all(bf16[2,128,1,4,1024]{4,3,1,2,0:T(4,128)(2,1)S(1)} %pad_maximum_fusion.1), channel_id=1, replica_groups=mesh['dp'=128,'rep'=2] {'rep'}, dimensions={0} | all-to-all | bytes 4194304 | tf_op jit(solution)/shard_map/all_to_all | solution.py:13
  83.9 2.6 %copy.10 = bf16[128,2,1,4,1024]{4,3,1,0,2:T(4,128)(2,1)} copy(bf16[128,2,1,4,1024]{4,3,0,2,1:T(4,128)(2,1)S(1)} %bitcast.50) | data formatting | bytes 4194304 | tf_op jit(solution)/shard_map/reshape | solution.py:14
  86.5 2.5 %reshape_reshape.3 = bf16[1024,1024]{1,0:T(8,128)(2,1)S(1)} reshape(bf16[128,2,1,4,1024]{4,3,1,0,2:T(4,128)(2,1)} %copy.10) | data formatting | bytes 4194304 | tf_op jit(solution)/shard_map/reshape;reshape | solution.py:47
  91.2 1.7 %fusion.18 = f32[1,1024]{1,0:T(1,128)S(1)} fusion(bf16[1024,1024]{1,0:T(8,128)(2,1)S(1)} %reshape_reshape.3, f32[1024,1]{0,1:T(1,128)S(1)} %bitcast.60), kind=kOutput, calls=%fused_computation.53 | convolution fusion | flops 12582912 | bytes 2105344 | tf_op jit(solution)/shard_map/dot_general | solution.py:84
  92.9 0.6 broadcast_select_fusion
  93.6 0.6 convert_reduce_fusion
  95.7 4.4 %sort.17 = (s32[1024]{0:T(1024)}, s32[1024]{0:T(1024)S(1)}) sort(s32[1024]{0:T(1024)S(1)} %get-tuple-element.75, s32[1024]{0:T(1024)S(1)} %iota.25), dimensions={0}, to_apply=%region_5.6 | sort | flops 10240 | bytes 16384 | tf_op jit(solution)/shard_map/jit(argsort)/sort | solution.py:59
  100.0 2.3 %gather_fusion = s32[512]{0:T(512)S(1)} fusion(s32[1024]{0:T(1024)S(1)} %get-tuple-element.40, s32[1024]{0:T(1024)S(1)} %pad_clamp_fusion.1), kind=kCustom, calls=%fused_computation | custom fusion | bytes 6144 | tf_op jit(solution)/shard_map/gather | solution.py:61
  102.4 2.1 %gather_fusion.1 = bf16[512,1024]{1,0:T(8,128)(2,1)S(1)} fusion(bf16[1024,1024]{1,0:T(8,128)(2,1)S(1)} %reshape_reshape.3, s32[1024]{0:T(1024)S(1)} %pad_clamp_fusion), kind=kCustom, calls=%fused_computation.1 | custom fusion | bytes 2099200 | tf_op jit(solution)/shard_map/gather | solution.py:62
  104.4 1.1 fusion.17
  105.5 4.3 %collective-permute-start = (bf16[256,1024]{1,0:T(8,128)(2,1)}, bf16[256,1024]{1,0:T(8,128)(2,1)S(1)}, u32[]{:S(2)}, u32[]{:S(2)}) collective-permute-start(bf16[256,1024]{1,0:T(8,128)(2,1)} %get-tuple-element.72), channel_id=1, source_target_pairs={{0,1},{1,2},{2,3},{3,4},{4,5},{5,6},{6,7},{7,8},{8,9},{9,10},{10,1... | collective-permute-start | bytes 1572872 | tf_op jit(solution)/shard_map/ppermute | solution.py:23
  109.8 1.9 %collective-permute-start.1 = (bf16[256,1024]{1,0:T(8,128)(2,1)}, bf16[256,1024]{1,0:T(8,128)(2,1)S(1)}, u32[]{:S(2)}, u32[]{:S(2)}) collective-permute-start(bf16[256,1024]{1,0:T(8,128)(2,1)} %get-tuple-element.73), channel_id=1, source_target_pairs={{1,0},{2,1},{3,2},{4,3},{5,4},{6,5},{7,6},{8,7},{9,8},{10,9},{11,1... | collective-permute-start | bytes 1572872 | tf_op jit(solution)/shard_map/ppermute | solution.py:23
  111.8 4.4 %collective-permute-done = bf16[256,1024]{1,0:T(8,128)(2,1)S(1)} collective-permute-done((bf16[256,1024]{1,0:T(8,128)(2,1)}, bf16[256,1024]{1,0:T(8,128)(2,1)S(1)}, u32[]{:S(2)}, u32[]{:S(2)}) %collective-permute-start) | collective-permute-done | bytes 524320 | tf_op jit(solution)/shard_map/ppermute | solution.py:23
  116.2 6.4 %collective-permute-done.1 = bf16[256,1024]{1,0:T(8,128)(2,1)S(1)} collective-permute-done((bf16[256,1024]{1,0:T(8,128)(2,1)}, bf16[256,1024]{1,0:T(8,128)(2,1)S(1)}, u32[]{:S(2)}, u32[]{:S(2)}) %collective-permute-start.1) | collective-permute-done | bytes 524320 | tf_op jit(solution)/shard_map/ppermute | solution.py:23
  122.6 1.9 %pad_maximum_fusion = bf16[1536,1024]{1,0:T(8,128)(2,1)} fusion(bf16[256,1024]{1,0:T(8,128)(2,1)S(1)} %collective-permute-done.1, bf16[256,1024]{1,0:T(8,128)(2,1)S(1)} %collective-permute-done, bf16[1024,1024]{1,0:T(8,128)(2,1)S(1)} %reshape_reshape.3), kind=kLoop, calls=%fused_computation.13 | loop fusion | flops 9437184 | bytes 6291456 | tf_op jit(solution)/shard_map/concatenate | solution.py:65
  124.5 13.6 %while.11 = (s32[]{:T(128)}, f32[2,512]{1,0:T(2,128)S(1)}, pred[1536]{0:T(1024)(128)(4,1)S(1)}, s32[2]{0:T(128)S(1)}, bf16[1024,1024]{1,0:T(8,128)(2,1)S(1)}, /*...) while((s32[]{:T(128)}, f32[2,512]{1,0:T(2,128)S(1)}, ...), condition=%wide.region_9.10_spmd.clone, body=%wide.region_7.9_spmd.clone.sunk | while | flops 1613758464 | bytes 4206743 | solution.py:82
  127.3 4.0 %fusion.28 = f32[512]{0:T(512)S(1)} fusion(bf16[1536,1024]{1,0:T(8,128)(2,1)} %get-tuple-element.136, s32[512]{0:T(512)S(1)} %iota_add_fusion.2, pred[1536]{0:T(1024)(128)(4,1)S(1)} %get-tuple-element.133, bf16[1024,1024]{1,0:T(8,128)(2,1)S(1)} %get-tuple-element.135, s32[]{:T(128)S(6)} %select_n.86), kind=kOutput, calls=%fused_computation.7.clone.1 | convolution fusion | flops 1613757952 | bytes 4200452 | tf_op jit(solution)/shard_map/while/body/eval_jaxpr/dot_general | solution.py:74
  134.1 4.0 %fusion.28 = f32[512]{0:T(512)S(1)} fusion(bf16[1536,1024]{1,0:T(8,128)(2,1)} %get-tuple-element.136, s32[512]{0:T(512)S(1)} %iota_add_fusion.2, pred[1536]{0:T(1024)(128)(4,1)S(1)} %get-tuple-element.133, bf16[1024,1024]{1,0:T(8,128)(2,1)S(1)} %get-tuple-element.135, s32[]{:T(128)S(6)} %select_n.86), kind=kOutput, calls=%fused_computation.7.clone.1 | convolution fusion | flops 1613757952 | bytes 4200452 | tf_op jit(solution)/shard_map/while/body/eval_jaxpr/dot_general | solution.py:74
  (42 shorter events, 5.4 us)
Async XLA Ops:
  0.6 1.4 copy-start.1
  0.6 1.6 %copy-start = (f32[512,1024]{1,0:T(8,128)S(1)}, f32[512,1024]{1,0:T(8,128)}, u32[]{:S(2)}) copy-start(f32[512,1024]{1,0:T(8,128)} %param.5) | copy-start | bytes 6291460
  89.4 6.1 %copy-start.2 = (s32[1,2,256]{2,1,0:T(2,128)S(1)}, s32[1,2,256]{2,1,0:T(2,128)}, u32[]{:S(2)}) copy-start(s32[1,2,256]{2,1,0:T(2,128)} %param.7) | copy-start | bytes 6148
  105.5 10.8 %collective-permute-start = (bf16[256,1024]{1,0:T(8,128)(2,1)}, bf16[256,1024]{1,0:T(8,128)(2,1)S(1)}, u32[]{:S(2)}, u32[]{:S(2)}) collective-permute-start(bf16[256,1024]{1,0:T(8,128)(2,1)} %get-tuple-element.72), channel_id=1, source_target_pairs={{0,1},{1,2},{2,3},{3,4},{4,5},{5,6},{6,7},{7,8},{8,9},{9,10},{10,1... | collective-permute-start | bytes 1572872 | tf_op jit(solution)/shard_map/ppermute | solution.py:23
  109.8 12.8 %collective-permute-start.1 = (bf16[256,1024]{1,0:T(8,128)(2,1)}, bf16[256,1024]{1,0:T(8,128)(2,1)S(1)}, u32[]{:S(2)}, u32[]{:S(2)}) collective-permute-start(bf16[256,1024]{1,0:T(8,128)(2,1)} %get-tuple-element.73), channel_id=1, source_target_pairs={{1,0},{2,1},{3,2},{4,3},{5,4},{6,5},{7,6},{8,7},{9,8},{10,9},{11,1... | collective-permute-start | bytes 1572872 | tf_op jit(solution)/shard_map/ppermute | solution.py:23
